TPU v7x, 32 devices: a whole 2x2x4 slice. The times are simulated.
32 devices in a mesh: fsdp: 8 (over y, x, core), sp: 4 (over z).
Axes of the slice: x: 2, y: 2, z: 4, core: 2. Of those that a mesh axis runs over, the one named last changes fastest.
Arguments:
- hidden_in: bfloat16 [8, 1024, 2048], P('fsdp', 'sp'), may hold values from -6 to 6
- segments: int32 [8, 1024], P('fsdp'), may hold values from 0 to 3, never falling along the last dimension, each value on 1 to 640 neighbouring positions
- ln1_gain: float32 [2048], replicated, may hold values from 0.5 to 1.5
- ln1_bias: float32 [2048], replicated, may hold values from -1 to 1
- ln2_gain: float32 [2048], replicated, may hold values from 0.5 to 1.5
- ln2_bias: float32 [2048], replicated, may hold values from -1 to 1
- w_qkv: bfloat16 [6144, 2048], P('fsdp'), may hold values from -0.125 to 0.125
- b_qkv: float32 [6144], replicated, may hold values from -1 to 1
- w_dense: bfloat16 [2048, 2048], P('fsdp'), may hold values from -0.75 to 0.75
- b_dense: float32 [2048], replicated, may hold values from -1 to 1
- w_up: bfloat16 [8192, 2048], P('fsdp'), may hold values from -0.125 to 0.125
- b_up: float32 [8192], replicated, may hold values from -1 to 1
- w_down: bfloat16 [8192, 2048], P('fsdp'), may hold values from -0.0625 to 0.0625
- b_down: float32 [2048], replicated, may hold values from -1 to 1
- cotangent: bfloat16 [8, 1024, 2048], P('fsdp', 'sp'), may hold values from -6 to 6
Outputs:
- output: bfloat16 [8, 1024, 2048], P('fsdp', 'sp')
- input_grad: bfloat16 [8, 1024, 2048], P('fsdp', 'sp')
- grad_ln1_gain: float32 [2048], P('fsdp')
- grad_ln1_bias: float32 [2048], P('fsdp')
- grad_ln2_gain: float32 [2048], P('fsdp')
- grad_ln2_bias: float32 [2048], P('fsdp')
- grad_w_qkv: float32 [6144, 2048], P('fsdp')
- grad_b_qkv: float32 [6144], P('fsdp')
- grad_w_dense: float32 [2048, 2048], P('fsdp')
- grad_b_dense: float32 [2048], P('fsdp')
- grad_w_up: float32 [8192, 2048], P('fsdp')
- grad_b_up: float32 [8192], P('fsdp')
- grad_w_down: float32 [8192, 2048], P('fsdp')
- grad_b_down: float32 [2048], P('fsdp')
Inputs may be any that keep to these rules, and one draw needn't show every extreme that they name: `segments`: along each sequence the segment numbers never fall; each document is one run of 1 to 640 positions, and some document has exactly 640.
All inputs are finite; a program needn't handle non-finite values.
Results may differ from a plain program's by a relative error of at most 0.011.
Values may be sent and summed in bfloat16 or wider, within the bound.
A program may use at most 704 MiB of HBM per device.

v0:
```python
import math
import jax
import jax.numpy as jnp
from jax import lax
from jax.sharding import PartitionSpec as P

HEADS = 8
HEAD_DIM = 256
ROT = 64
EPSILON = 1e-05
NEGATIVE = -1e30
ROOT_HALF = 0.7071067811865476
ROOT_TWO_PI = 2.5066282746310002


def contract_rows(former, latter):
    return lax.dot_general(
        former, latter, (((0,), (0,)), ((), ())), preferred_element_type=jnp.float32
    )


def times_transposed(former, latter):
    return lax.dot_general(
        former, latter, (((1,), (1,)), ((), ())), preferred_element_type=jnp.float32
    )


def norm_forward(inputs, norm_gain, norm_shift):
    average = jnp.mean(inputs, axis=-1, keepdims=True)
    centred = inputs - average
    variance = jnp.mean(centred * centred, axis=-1, keepdims=True)
    inverse = lax.rsqrt(variance + EPSILON)
    scaled = centred * inverse
    return (scaled * norm_gain + norm_shift, scaled, inverse)


def norm_backward(upstream, scaled, inverse, norm_gain):
    weighted = upstream * norm_gain
    first_mean = jnp.mean(weighted, axis=-1, keepdims=True)
    second_mean = jnp.mean(weighted * scaled, axis=-1, keepdims=True)
    input_part = inverse * (weighted - first_mean - scaled * second_mean)
    return (input_part, jnp.sum(upstream * scaled, axis=0), jnp.sum(upstream, axis=0))


def gelu_pair(hidden):
    cumulative = 0.5 * (1.0 + jax.scipy.special.erf(hidden * ROOT_HALF))
    return (
        hidden * cumulative,
        cumulative + hidden * jnp.exp(-0.5 * hidden * hidden) / ROOT_TWO_PI,
    )


def rotary_tables(segment_rows):
    length = segment_rows.shape[-1]
    places = jnp.arange(length, dtype=jnp.int32)
    changes = jnp.concatenate(
        [
            jnp.ones_like(segment_rows[..., :1]),
            (segment_rows[..., 1:] != segment_rows[..., :-1]).astype(jnp.int32),
        ],
        axis=-1,
    )
    first_place = lax.cummax(changes * places, axis=segment_rows.ndim - 1)
    position = (places - first_place).astype(jnp.float32)
    exponent = jnp.arange(0, ROT, 2).astype(jnp.float32) / ROT
    frequency = 1.0 / jnp.power(10000.0, exponent)
    angles = position[..., None] * frequency
    angles = jnp.concatenate([angles, angles], axis=-1)
    return (jnp.cos(angles), jnp.sin(angles))


def rotate(heads_part, cos_table, sin_table):
    half_rot = ROT // 2
    turned = heads_part[..., :ROT]
    swapped = jnp.concatenate([-turned[..., half_rot:], turned[..., :half_rot]], axis=-1)
    turned = turned * cos_table[..., None, :] + swapped * sin_table[..., None, :]
    return jnp.concatenate([turned, heads_part[..., ROT:]], axis=-1)


def unrotate(grads_part, cos_table, sin_table):
    half_rot = ROT // 2
    turned = grads_part[..., :ROT]
    along_sin = turned * sin_table[..., None, :]
    back_turn = jnp.concatenate([along_sin[..., half_rot:], -along_sin[..., :half_rot]], axis=-1)
    turned = turned * cos_table[..., None, :] + back_turn
    return jnp.concatenate([turned, grads_part[..., ROT:]], axis=-1)


def build_mask(segment_row):
    places = jnp.arange(segment_row.shape[0], dtype=jnp.int32)
    return (segment_row[:, None] == segment_row[None, :]) & (places[None, :] <= places[:, None])


def attend_forward(scanned):
    queries, keys_rot, values, segment_row = scanned
    scores = jnp.einsum("qhd,khd->hqk", queries, keys_rot, preferred_element_type=jnp.float32) * (
        1.0 / math.sqrt(HEAD_DIM)
    )
    scores = jnp.where(build_mask(segment_row)[None], scores, NEGATIVE)
    row_top = jnp.max(scores, axis=-1, keepdims=True)
    exponent = jnp.exp(scores - row_top)
    row_total = jnp.sum(exponent, axis=-1, keepdims=True)
    attention = (exponent / row_total).astype(jnp.bfloat16)
    context = jnp.einsum("hqk,khd->qhd", attention, values, preferred_element_type=jnp.float32)
    return (context.astype(jnp.bfloat16), row_top + jnp.log(row_total))


def attend_backward(scanned):
    queries, keys_rot, values, segment_row, log_total, context_grad = scanned
    scale_factor = 1.0 / math.sqrt(HEAD_DIM)
    scores = (
        jnp.einsum("qhd,khd->hqk", queries, keys_rot, preferred_element_type=jnp.float32)
        * scale_factor
    )
    attention = jnp.where(build_mask(segment_row)[None], jnp.exp(scores - log_total), 0.0)
    value_grad = jnp.einsum(
        "hqk,qhd->khd",
        attention.astype(jnp.bfloat16),
        context_grad,
        preferred_element_type=jnp.float32,
    )
    attention_grad = jnp.einsum(
        "qhd,khd->hqk", context_grad, values, preferred_element_type=jnp.float32
    )
    row_centre = jnp.sum(attention * attention_grad, axis=-1, keepdims=True)
    score_grad = (attention * (attention_grad - row_centre)).astype(jnp.bfloat16)
    query_grad = (
        jnp.einsum("hqk,khd->qhd", score_grad, keys_rot, preferred_element_type=jnp.float32)
        * scale_factor
    )
    key_grad = (
        jnp.einsum("hqk,qhd->khd", score_grad, queries, preferred_element_type=jnp.float32)
        * scale_factor
    )
    return (query_grad, key_grad, value_grad)


def per_device(
    hidden_in,
    segments,
    ln1_gain,
    ln1_bias,
    ln2_gain,
    ln2_bias,
    w_qkv,
    b_qkv,
    w_dense,
    b_dense,
    w_up,
    b_up,
    w_down,
    b_down,
    cotangent,
):
    seq_count, shard_len, width = hidden_in.shape
    tok_rows = seq_count * shard_len
    inputs = hidden_in.reshape(tok_rows, width).astype(jnp.float32)
    upstream = cotangent.reshape(tok_rows, width)
    upstream_f32 = upstream.astype(jnp.float32)
    full_qkv, full_dense = (
        lax.all_gather(w_qkv, "fsdp", axis=0, tiled=True),
        lax.all_gather(w_dense, "fsdp", axis=0, tiled=True),
    )
    normed, scaled_attn, inverse_attn = norm_forward(inputs, ln1_gain, ln1_bias)
    normed = normed.astype(jnp.bfloat16)
    packed = (times_transposed(normed, full_qkv) + b_qkv).astype(jnp.bfloat16)
    packed = packed.reshape(seq_count, shard_len, HEADS, 3 * HEAD_DIM)
    by_head = lax.all_to_all(packed, "sp", split_axis=2, concat_axis=1, tiled=True)
    cos_table, sin_table = rotary_tables(segments)
    queries = rotate(by_head[..., :HEAD_DIM].astype(jnp.float32), cos_table, sin_table).astype(
        jnp.bfloat16
    )
    keys_rot = rotate(
        by_head[..., HEAD_DIM : 2 * HEAD_DIM].astype(jnp.float32), cos_table, sin_table
    ).astype(jnp.bfloat16)
    values = by_head[..., 2 * HEAD_DIM :]
    context, log_total = lax.map(attend_forward, (queries, keys_rot, values, segments))
    merged = lax.all_to_all(context, "sp", split_axis=1, concat_axis=2, tiled=True).reshape(
        tok_rows, width
    )
    attended = times_transposed(merged, full_dense) + b_dense
    normed_mlp, scaled_mlp, inverse_mlp = norm_forward(inputs, ln2_gain, ln2_bias)
    normed_mlp = normed_mlp.astype(jnp.bfloat16)
    full_up, full_down = (
        lax.all_gather(w_up, "fsdp", axis=0, tiled=True),
        lax.all_gather(w_down, "fsdp", axis=0, tiled=True),
    )
    hidden = times_transposed(normed_mlp, full_up) + b_up
    activated, slope = gelu_pair(hidden)
    activated = activated.astype(jnp.bfloat16)
    mlp_out = jnp.dot(activated, full_down, preferred_element_type=jnp.float32) + b_down
    hidden_grad = (times_transposed(upstream, full_down) * slope).astype(jnp.bfloat16)
    mlp_in_grad = jnp.dot(hidden_grad, full_up, preferred_element_type=jnp.float32)
    grad_cols = hidden_grad
    mlp_shard = lax.psum_scatter(
        jnp.concatenate(
            [contract_rows(grad_cols, normed_mlp), contract_rows(activated, upstream)], axis=1
        ),
        "fsdp",
        scatter_dimension=0,
        tiled=True,
    )
    up_grad = mlp_shard[:, :width]
    down_grad = mlp_shard[:, width:]
    bias_up = jnp.sum(hidden_grad.astype(jnp.float32), axis=0)
    output = (inputs + attended + mlp_out).astype(jnp.bfloat16).reshape(seq_count, shard_len, width)
    dense_in_grad = jnp.dot(upstream, full_dense, preferred_element_type=jnp.float32).astype(
        jnp.bfloat16
    )
    context_grad = lax.all_to_all(
        dense_in_grad.reshape(seq_count, shard_len, HEADS, HEAD_DIM),
        "sp",
        split_axis=2,
        concat_axis=1,
        tiled=True,
    )
    query_grad, key_grad, value_grad = lax.map(
        attend_backward, (queries, keys_rot, values, segments, log_total, context_grad)
    )
    packed_grad = jnp.concatenate(
        [
            unrotate(query_grad, cos_table, sin_table),
            unrotate(key_grad, cos_table, sin_table),
            value_grad,
        ],
        axis=-1,
    ).astype(jnp.bfloat16)
    packed_grad = lax.all_to_all(
        packed_grad, "sp", split_axis=1, concat_axis=2, tiled=True
    ).reshape(tok_rows, 3 * width)
    normed_grad = jnp.dot(packed_grad, full_qkv, preferred_element_type=jnp.float32)
    qkv_part = w_qkv.shape[0]
    dense_part = w_dense.shape[0]
    block_size = qkv_part + dense_part
    block_total = lax.axis_size("fsdp") * block_size // block_size
    grad_cols = packed_grad
    qkv_term = contract_rows(grad_cols, normed).reshape(block_total, qkv_part, width)
    dense_term = contract_rows(upstream, merged).reshape(block_total, dense_part, width)
    attn_shard = lax.psum_scatter(
        jnp.concatenate([qkv_term, dense_term], axis=1).reshape(
            lax.axis_size("fsdp") * block_size, width
        ),
        "fsdp",
        scatter_dimension=0,
        tiled=True,
    )
    qkv_local = attn_shard[:qkv_part]
    dense_local = attn_shard[qkv_part:]
    grad_qkv_w, grad_dense_w, grad_up_w, grad_down_w = lax.psum(
        (qkv_local, dense_local, up_grad, down_grad), "sp"
    )
    attn_input, gain_one, shift_one = norm_backward(
        normed_grad, scaled_attn, inverse_attn, ln1_gain
    )
    mlp_input, gain_two, shift_two = norm_backward(mlp_in_grad, scaled_mlp, inverse_mlp, ln2_gain)
    input_grad = (
        (upstream_f32 + attn_input + mlp_input)
        .astype(jnp.bfloat16)
        .reshape(seq_count, shard_len, width)
    )
    bias_out = jnp.sum(upstream_f32, axis=0)
    bias_qkv = jnp.sum(packed_grad.astype(jnp.float32), axis=0)
    summed = lax.psum(
        (gain_one, shift_one, gain_two, shift_two, bias_qkv, bias_out, bias_up), ("fsdp", "sp")
    )
    fsdp_index = lax.axis_index("fsdp")
    fsdp_count = lax.axis_size("fsdp")

    def own_part(vector):
        piece_len = vector.shape[0] // fsdp_count
        return lax.dynamic_slice_in_dim(vector, fsdp_index * piece_len, piece_len, 0)

    bias_out_part = own_part(summed[5])
    return (
        output,
        input_grad,
        own_part(summed[0]),
        own_part(summed[1]),
        own_part(summed[2]),
        own_part(summed[3]),
        grad_qkv_w,
        own_part(summed[4]),
        grad_dense_w,
        bias_out_part,
        grad_up_w,
        own_part(summed[6]),
        grad_down_w,
        bias_out_part,
    )


def solution(mesh):
    return jax.shard_map(
        per_device,
        mesh=mesh,
        in_specs=(
            P("fsdp", "sp", None),
            P("fsdp", None),
            P(),
            P(),
            P(),
            P(),
            P("fsdp", None),
            P(),
            P("fsdp", None),
            P(),
            P("fsdp", None),
            P(),
            P("fsdp", None),
            P(),
            P("fsdp", "sp", None),
        ),
        out_specs=(
            P("fsdp", "sp", None),
            P("fsdp", "sp", None),
            P("fsdp"),
            P("fsdp"),
            P("fsdp"),
            P("fsdp"),
            P("fsdp", None),
            P("fsdp"),
            P("fsdp", None),
            P("fsdp"),
            P("fsdp", None),
            P("fsdp"),
            P("fsdp", None),
            P("fsdp"),
        ),
        check_vma=False,
    )
```

profile of v0, /device:TPU:0, one launch (start us, length us, event | category | flops | bytes accessed | tf_op | source)
XLA Modules:
  0.0 2658.6 jit_solution(7697553967098281096)
XLA Ops:
  10.7 56.3 %all-gather.7.cloned.1.call-done = bf16[2048,2048]{1,0:T(8,128)(2,1)} async-done(((bf16[256,2048]{1,0:T(8,128)(2,1)}), bf16[2048,2048]{1,0:T(8,128)(2,1)}) %all-gather.7.cloned.1.call-update) | async-done | bytes 8388624 | tf_op jit(solution)/shard_map/all_gather | solution.py:162
  67.0 5.7 convolution_convert_fusion
  74.3 4.6 all-to-all-start.2
  78.9 115.4 %all-gather.5.cloned.1.call-done = bf16[6144,2048]{1,0:T(8,128)(2,1)} async-done(((bf16[768,2048]{1,0:T(8,128)(2,1)}), bf16[6144,2048]{1,0:T(8,128)(2,1)}) %all-gather.5.cloned.1.call-update) | async-done | bytes 25165840 | tf_op jit(solution)/shard_map/all_gather | solution.py:161
  194.3 12.9 fusion.5
  207.1 3.3 copy.178
  210.4 2.3 copy.141
  213.7 5.0 all-to-all-start
  219.9 2.9 fusion.90
  224.4 2.3 copy.149
  226.6 63.2 %all-to-all-done = bf16[1,256,8,768]{3,1,0,2:T(8,128)(2,1)S(1)} async-done(((bf16[1,256,8,768]{3,1,0,2:T(8,128)(2,1)}), bf16[1,256,8,768]{3,1,0,2:T(8,128)(2,1)S(1)}, u32[]{:S(2)}, u32[]{:S(2)}) %all-to-all-start) | async-done | bytes 3145760 | tf_op jit(solution)/shard_map/all_to_all | solution.py:168
  297.8 2.5 select_reduce_fusion
  303.7 4.0 fusion.60
  307.7 3.7 copy.145
  311.4 4.4 all-to-all-start.1
  315.9 5.8 multiply_reduce_fusion
  322.8 2.6 multiply_convert_fusion
  331.2 4.5 multiply_bitcast_fusion
  338.5 2.2 copy.161
  351.8 7.4 fusion.57
  359.1 8.8 copy.162
  368.0 5.2 all-to-all-start.3
  375.5 8.1 fusion.73
  383.6 59.0 %all-to-all-done.3 = bf16[1,1024,2,768]{3,2,0,1:T(2,128)(2,1)} async-done(((bf16[1,1024,2,768]{3,2,0,1:T(2,128)(2,1)}), bf16[1,1024,2,768]{3,2,0,1:T(2,128)(2,1)}, u32[]{:S(2)}, u32[]{:S(2)}) %all-to-all-start.3) | async-done | bytes 3145760 | tf_op jit(solution)/shard_map/all_to_all | solution.py:228
  442.7 2.3 copy.163
  445.0 3.2 copy.164
  448.2 21.9 fusion.62
  470.1 45.9 %pad_maximum_fusion.1 = f32[8,1024,2048]{2,1,0:T(8,128)} fusion(f32[8,256,2048]{2,1,0:T(8,128)} %bitcast.181, f32[8,768,2048]{2,1,0:T(8,128)} %fusion.62), kind=kLoop, calls=%fused_computation.1 | loop fusion | flops 16777216 | bytes 134217728 | tf_op jit(solution)/shard_map/concatenate | solution.py:240
  517.4 20.7 convolution_add_fusion
  538.1 27.3 %convert_reduce_fusion = (f32[8192]{0:T(1024)}, bf16[256,8192]{1,0:T(8,128)(2,1)}) fusion(f32[256,8192]{1,0:T(8,128)} %convolution_add_fusion, bf16[8192,2048]{1,0:T(8,128)(2,1)} %all-gather.11.cloned.1.call-done, bf16[1,256,2048]{2,1,0:T(8,128)(2,1)S(1)} %copy-done.11), kind=kOutput, calls=%fused_computation.10 | convolution fusion | flops 8615092224 | bytes 47218688 | tf_op jit(solution)/shard_map/dot_general | solution.py:23
  565.4 40.8 %fusion.101 = f32[8192,2048]{0,1:T(8,128)} fusion(bf16[256,8192]{1,0:T(8,128)(2,1)} %get-tuple-element.202, bf16[1,256,2048]{2,1,0:T(8,128)(2,1)S(1)} %copy-done.4, f32[2048]{0:T(1024)S(1)} %copy-done.45, f32[2048]{0:T(1024)S(1)} %copy-done.38, f32[256]{0:T(256)S(1)} %add_rsqrt_fusion, f32[256]{0:T(256)S(1)} %broadcast_multiply_fusion.5), kind=kOutput, calls=%fused_computation.162 | convolution fusion | flops 8593080320 | bytes 72370176 | tf_op jit(solution)/shard_map/dot_general | solution.py:17
  606.2 29.2 %fusion.71 = f32[8192,2048]{0,1:T(8,128)} fusion(bf16[1,256,2048]{2,1,0:T(8,128)(2,1)S(1)} %copy-done.11, f32[256,8192]{1,0:T(8,128)} %convolution_add_fusion), kind=kOutput, calls=%fused_computation.110 | convolution fusion | flops 8600420352 | bytes 76546048 | tf_op jit(solution)/shard_map/dot_general | solution.py:17
  635.5 90.6 %pad_maximum_fusion = f32[8192,4096]{0,1:T(8,128)} fusion(f32[8192,2048]{0,1:T(8,128)} %fusion.71, f32[8192,2048]{0,1:T(8,128)} %fusion.101), kind=kLoop, calls=%fused_computation | loop fusion | flops 33554432 | bytes 268435456 | tf_op jit(solution)/shard_map/concatenate | solution.py:196
  729.3 17.5 fusion.107
  746.9 13.7 fusion.43
  760.7 3.1 convert_reduce_fusion.3
  763.9 142.9 %reduce-scatter.3.cloned.1.call-done = f32[1024,2048]{1,0:T(8,128)} async-done(((f32[8192,2048]{1,0:T(8,128)}), f32[1024,2048]{1,0:T(8,128)}) %reduce-scatter.3.cloned.1.call-update) | async-done | bytes 8388624 | tf_op jit(solution)/shard_map/reduce_scatter | solution.py:239
  906.8 3.1 slice.138
  909.9 6.3 slice.137
  916.2 735.3 %reduce-scatter.5.cloned.1.call-done = f32[1024,4096]{0,1:T(8,128)} async-done(((f32[8192,4096]{0,1:T(8,128)}), f32[1024,4096]{0,1:T(8,128)}) %reduce-scatter.5.cloned.1.call-update) | async-done | bytes 16777232 | tf_op jit(solution)/shard_map/reduce_scatter | solution.py:195
  1651.5 11.3 fusion.104
  1664.0 7.1 fusion.16
  1671.2 23.5 fusion.30
  1694.7 88.5 %all-reduce.5.cloned.1.call-done = (f32[2048]{0:T(1024)}, f32[2048]{0:T(1024)}, f32[2048]{0:T(1024)}, f32[2048]{0:T(1024)}, f32[6144]{0:T(1024)}, /*index=5*/f32[2048]{0:T(1024)}, f32[8192]{0:T(1024)}) async-done(((f32[2048]{0:T(1024)}, f32[2048]{0:T(1024)}, f32[2048]{0:T(1024)}, f32[2048]{0:T(1024)}, f32[6144]{0:T(1024)}, /*index=5*/f32[2048]{0:T(1024)}, f32[8192]{0:T(1024)}), (f32[2048]{0:T(1024)}, ...) | async-done | bytes 98320 | tf_op jit(solution)/shard_map/psum | solution.py:263
  1791.8 833.2 %all-reduce.7.cloned.1.call-done = (f32[768,2048]{1,0:T(8,128)}, f32[256,2048]{1,0:T(8,128)}, f32[1024,2048]{0,1:T(8,128)}, f32[1024,2048]{0,1:T(8,128)}) async-done(((f32[768,2048]{1,0:T(8,128)}, f32[256,2048]{1,0:T(8,128)}, f32[1024,2048]{0,1:T(8,128)}, f32[1024,2048]{0,1:T(8,128)}), (f32[768,2048]{1,0:T(8,128)}, f32[256,2048]{1,0:T(8,128)}, f32[1024,2048]{0,1:T(8,128)}, ...) | async-done | bytes 25165840 | tf_op jit(solution)/shard_map/psum | solution.py:249
  2625.0 9.1 copy.166
  2634.1 9.1 copy.167
  2643.8 6.4 copy.197
  (184 shorter events, 59.1 us)
Async XLA Ops:
  7.2 59.8 %all-gather.7.cloned.1.call-start = ((), (), s32[]{:S(2)}) async-start(), calls=%async_computation.7 | async-start | bytes 9437184 | tf_op jit(solution)/shard_map/all_gather | solution.py:162
  7.9 186.4 %all-gather.5.cloned.1.call-start = ((), (), s32[]{:S(2)}) async-start(), calls=%async_computation.6 | async-start | bytes 28311552 | tf_op jit(solution)/shard_map/all_gather | solution.py:161
  8.7 507.5 %all-gather.9.cloned.1.call-start = ((), (), s32[]{:S(2)}) async-start(), calls=%async_computation.8 | async-start | bytes 37748736 | tf_op jit(solution)/shard_map/all_gather | solution.py:185
  9.4 57.6 %copy-start.9 = (bf16[1,256,2048]{2,1,0:T(8,128)(2,1)S(1)}, bf16[1,256,2048]{2,1,0:T(8,128)(2,1)}, u32[]{:S(2)}) copy-start(bf16[1,256,2048]{2,1,0:T(8,128)(2,1)} %param.29) | copy-start | bytes 3145732
  9.4 528.6 %all-gather.11.cloned.1.call-start = ((), (), s32[]{:S(2)}) async-start(), calls=%async_computation.9 | async-start | bytes 37748736 | tf_op jit(solution)/shard_map/all_gather | solution.py:186
  10.2 555.2 %copy-start.40 = (f32[256]{0:T(256)}, f32[256]{0:T(256)S(1)}, u32[]{:S(2)}) copy-start(f32[256]{0:T(256)S(1)} %broadcast_multiply_fusion.5) | copy-start | bytes 3076
  10.7 554.7 %copy-start.42 = (f32[256]{0:T(256)}, f32[256]{0:T(256)S(1)}, u32[]{:S(2)}) copy-start(f32[256]{0:T(256)S(1)} %add_rsqrt_fusion) | copy-start | bytes 3076
  72.7 121.5 %copy-start.36 = (f32[2048]{0:T(1024)S(1)}, f32[2048]{0:T(1024)}, u32[]{:S(2)}) copy-start(f32[2048]{0:T(1024)} %param.17) | copy-start | bytes 24580
  72.8 121.5 %copy-start.44 = (f32[2048]{0:T(1024)S(1)}, f32[2048]{0:T(1024)}, u32[]{:S(2)}) copy-start(f32[2048]{0:T(1024)} %param.18) | copy-start | bytes 24580
  72.8 121.5 %copy-start.48 = (f32[6144]{0:T(1024)S(1)}, f32[6144]{0:T(1024)}, u32[]{:S(2)}) copy-start(f32[6144]{0:T(1024)} %param.22) | copy-start | bytes 73732
  74.3 138.4 %all-to-all-start.2 = ((bf16[1,256,8,256]{3,1,0,2:T(8,128)(2,1)}), bf16[1,256,8,256]{3,1,0,2:T(8,128)(2,1)S(1)}, u32[]{:S(2)}, u32[]{:S(2)}) async-start(bf16[1,256,8,256]{3,1,0,2:T(8,128)(2,1)} %copy.148), calls=%async_computation.2 | async-start | bytes 2097152 | tf_op jit(solution)/shard_map/all_to_all | solution.py:210
  212.7 6.0 copy-start.35
  213.7 76.1 %all-to-all-start = ((bf16[1,256,8,768]{3,1,0,2:T(8,128)(2,1)}), bf16[1,256,8,768]{3,1,0,2:T(8,128)(2,1)S(1)}, u32[]{:S(2)}, u32[]{:S(2)}) async-start(bf16[1,256,8,768]{3,1,0,2:T(8,128)(2,1)} %copy.141), calls=%async_computation | async-start | bytes 6291456 | tf_op jit(solution)/shard_map/all_to_all | solution.py:168
  294.6 2.6 copy-start.25
  294.6 2.6 copy-start.33
  297.2 3.0 copy-start.30
  297.2 3.0 copy-start.34
  300.3 3.4 copy-start
  311.4 56.5 %all-to-all-start.1 = ((bf16[1,1024,2,256]{3,2,0,1:T(2,128)(2,1)}), bf16[1,1024,2,256]{3,2,0,1:T(2,128)(2,1)}, u32[]{:S(2)}, u32[]{:S(2)}) async-start(bf16[1,1024,2,256]{3,2,0,1:T(2,128)(2,1)} %copy.145), calls=%async_computation.1 | async-start | bytes 2097152 | tf_op jit(solution)/shard_map/all_to_all | solution.py:178
  315.9 5.8 slice-start
  315.9 6.7 slice-start.1
  315.9 6.9 copy-start.14
  322.8 4.6 copy-start.26
  322.8 4.6 copy-start.31
  331.2 9.4 copy-start.17
  343.8 5.4 copy-start.27
  345.1 5.7 copy-start.28
  345.1 6.6 copy-start.15
  347.4 4.4 copy-start.32
  368.0 7.5 copy-start.10
  368.0 74.7 %all-to-all-start.3 = ((bf16[1,1024,2,768]{3,2,0,1:T(2,128)(2,1)}), bf16[1,1024,2,768]{3,2,0,1:T(2,128)(2,1)}, u32[]{:S(2)}, u32[]{:S(2)}) async-start(bf16[1,1024,2,768]{3,2,0,1:T(2,128)(2,1)} %copy.162), calls=%async_computation.3 | async-start | bytes 6291456 | tf_op jit(solution)/shard_map/all_to_all | solution.py:228
  373.2 533.6 %reduce-scatter.3.cloned.1.call-start = ((), (), s32[]{:S(2)}) async-start(), calls=%async_computation.10 | async-start | bytes 75497472 | tf_op jit(solution)/shard_map/reduce_scatter | solution.py:239
  375.5 8.1 copy-start.22
  445.0 25.2 copy-start.1
  516.1 21.9 copy-start.11
  516.1 1135.4 %reduce-scatter.5.cloned.1.call-start = ((), (), s32[]{:S(2)}) async-start(), calls=%async_computation.11 | async-start | bytes 150994944 | tf_op jit(solution)/shard_map/reduce_scatter | solution.py:195
  726.1 1057.0 %all-reduce.5.cloned.1.call-start = ((), (), s32[]{:S(2)}) async-start(), calls=%async_computation.12 | async-start | bytes 196608 | tf_op jit(solution)/shard_map/psum | solution.py:263
  729.3 17.5 copy-start.5
  729.3 17.6 copy-start.7
  729.3 17.6 copy-start.37
  729.3 17.6 copy-start.39
  729.3 17.6 copy-start.41
  729.3 17.6 copy-start.43
  746.9 13.8 copy-start.12
  763.8 1861.1 %all-reduce.7.cloned.1.call-start = ((), (), s32[]{:S(2)}) async-start(), calls=%async_computation.13 | async-start | bytes 50331648 | tf_op jit(solution)/shard_map/psum | solution.py:249
  1664.0 7.1 copy-start.50
  1785.2 858.0 %copy-start.46 = (f32[256]{0:T(256)}, f32[256]{0:T(256)S(1)}, u32[]{:S(2)}) copy-start(f32[256]{0:T(256)S(1)} %dynamic_slice.49) | copy-start | bytes 3076
  2643.8 6.4 copy-start.29
  (17 other events, 24.5 us)
Sparse Core Ops, SparseCore 0:
  9.9 57.0 all-gather.6
  68.9 125.3 all-gather.4
  196.2 160.7 all-gather.8
  358.7 160.8 all-gather.10
  523.0 383.7 reduce-scatter.2
  910.6 740.8 reduce-scatter.4
  1659.1 124.0 all-reduce.4
  1787.2 837.7 all-reduce.6
where the time goes:
time: 2670 us; the launch traced here: 2660 us
  waiting for transfers between devices  2100 us (79%)
  matrix products  255 us (10%)
  other arithmetic  156 us (6%)
  local copies, waits for them, and re-layouts  117 us (4%)
    psum x1, waiting for transfers between devices, per_device(): lax.psum((qkv_local, dense_local, up_grad, down_grad), 'sp')  833 us
    reduce_scatter x1, waiting for transfers between devices, per_device(): lax.psum_scatter(jnp.concatenate([contract_rows(grad_cols, normed_mlp), c...  735 us
    reduce_scatter x1, waiting for transfers between devices, per_device(): lax.psum_scatter(jnp.concatenate([qkv_term, dense_term], axis=1).reshape(...  143 us
    all_gather x1, waiting for transfers between devices, per_device(): lax.all_gather(w_qkv, 'fsdp', axis=0, tiled=True)  115 us
    dot_general x4, matrix products, contract_rows(): lax.dot_general(former, latter, (((0,), (0,)), ((), ())), preferred_eleme...  100 us
    concatenate x1, other arithmetic, per_device(): jnp.concatenate([contract_rows(grad_cols, normed_mlp), contract_rows(acti...  90.6 us
    psum x1, waiting for transfers between devices, per_device(): lax.psum((gain_one, shift_one, gain_two, shift_two, bias_qkv, bias_out, b...  88.5 us
    dot_general x4, matrix products, times_transposed(): lax.dot_general(former, latter, (((1,), (1,)), ((), ())), preferred_eleme...  68 us
  transfers between devices with their start and end apart: 12, of which 8 were waited for; matrix products, arithmetic and copies ran while one was open for 18% of the time, Pallas kernels for 0%

commit v1 on v0

--- a/solution.py
+++ b/solution.py
@@ -11,6 +11,18 @@
 NEGATIVE = -1e30
 ROOT_HALF = 0.7071067811865476
 ROOT_TWO_PI = 2.5066282746310002
+
+
+def doubled_up(x, axis, dim):
+    ways, here, lap = (lax.axis_size(axis), lax.axis_index(axis), x.shape[dim])
+    line, have = (x, 1)
+    while have < ways:
+        line = jnp.concatenate(
+            [line, lax.ppermute(line, axis, [(d, (d - have) % ways) for d in range(ways)])],
+            axis=dim,
+        )
+        have = 2 * have
+    return jnp.roll(line, here * lap, axis=dim)
 
 
 def contract_rows(former, latter):
@@ -159,7 +171,7 @@
     upstream_f32 = upstream.astype(jnp.float32)
     full_qkv, full_dense = (
         lax.all_gather(w_qkv, "fsdp", axis=0, tiled=True),
-        lax.all_gather(w_dense, "fsdp", axis=0, tiled=True),
+        doubled_up(w_dense, "fsdp", 0),
     )
     normed, scaled_attn, inverse_attn = norm_forward(inputs, ln1_gain, ln1_bias)
     normed = normed.astype(jnp.bfloat16)

time: 2670 us -> 2760 us (1.034)
  waiting for transfers between devices: 2100 us -> 2170 us
    ppermute x0 -> x3, waiting for transfers between devices: none -> 248 us  [doubled_up(): lax.ppermute(line, axis, [(d, (d - have) % ways) for d in range(ways)])]
    all_gather x1, waiting for transfers between devices: 115 us -> 0.01 us  [per_device(): lax.all_gather(w_qkv, 'fsdp', axis=0, tiled=True)]
    all_gather x1 -> x0, waiting for transfers between devices: 56.3 us -> none  [per_device(): lax.all_gather(w_dense, 'fsdp', axis=0, tiled=True)]
    unnamed x117 -> x133, local copies, waits for them, and re-layouts: 49.9 us -> 55.5 us
  transfers between devices with their start and end apart: 12 -> 14, of which waited for: 8 -> 10; matrix products, arithmetic and copies ran while one was open for 18% -> 18% of each run, Pallas kernels for 0% -> 0%
where the time goes in v1:
time: 2760 us; the launch traced here: 2750 us
  waiting for transfers between devices  2170 us (79%)
  matrix products  257 us (9%)
  other arithmetic  158 us (6%)
  local copies, waits for them, and re-layouts  124 us (4%)
    psum x1, waiting for transfers between devices, per_device(): lax.psum((qkv_local, dense_local, up_grad, down_grad), 'sp')  833 us
    reduce_scatter x1, waiting for transfers between devices, per_device(): lax.psum_scatter(jnp.concatenate([contract_rows(grad_cols, normed_mlp), c...  735 us
    ppermute x3, waiting for transfers between devices, doubled_up(): lax.ppermute(line, axis, [(d, (d - have) % ways) for d in range(ways)])  248 us
    reduce_scatter x1, waiting for transfers between devices, per_device(): lax.psum_scatter(jnp.concatenate([qkv_term, dense_term], axis=1).reshape(...  134 us
    dot_general x4, matrix products, contract_rows(): lax.dot_general(former, latter, (((0,), (0,)), ((), ())), preferred_eleme...  100 us
    concatenate x1, other arithmetic, per_device(): jnp.concatenate([contract_rows(grad_cols, normed_mlp), contract_rows(acti...  91.1 us
    psum x1, waiting for transfers between devices, per_device(): lax.psum((gain_one, shift_one, gain_two, shift_two, bias_qkv, bias_out, b...  88.6 us
    dot_general x4, matrix products, times_transposed(): lax.dot_general(former, latter, (((1,), (1,)), ((), ())), preferred_eleme...  70.7 us
  transfers between devices with their start and end apart: 14, of which 10 were waited for; matrix products, arithmetic and copies ran while one was open for 18% of the time, Pallas kernels for 0%

profile of v1, /device:TPU:0, one launch (start us, length us, event | category | flops | bytes accessed | tf_op | source)
XLA Modules:
  0.0 2746.5 jit_solution(5606445623455034644)
XLA Ops:
  9.4 3.4 collective-permute-start
  12.8 15.6 collective-permute-done
  28.7 75.6 %collective-permute-done.1 = bf16[512,2048]{1,0:T(8,128)(2,1)S(1)} collective-permute-done((bf16[512,2048]{1,0:T(8,128)(2,1)S(1)}, bf16[512,2048]{1,0:T(8,128)(2,1)S(1)}, u32[]{:S(2)}, u32[]{:S(2)}) %collective-permute-start.1) | collective-permute-done | bytes 2097184 | tf_op jit(solution)/shard_map/ppermute | solution.py:21
  104.2 3.3 pad_maximum_fusion.2
  110.3 157.1 %collective-permute-done.2 = bf16[1024,2048]{1,0:T(8,128)(2,1)} collective-permute-done((bf16[1024,2048]{1,0:T(8,128)(2,1)}, bf16[1024,2048]{1,0:T(8,128)(2,1)}, u32[]{:S(2)}, u32[]{:S(2)}) %collective-permute-start.2) | collective-permute-done | bytes 4194336 | tf_op jit(solution)/shard_map/ppermute | solution.py:21
  267.4 3.5 constant_dynamic-update-slice_fusion.4
  273.9 4.3 fusion.30
  279.9 4.9 all-to-all-start.2
  284.8 12.9 fusion.5
  297.7 2.8 copy.178
  302.8 6.8 all-to-all-done.2
  310.5 4.2 all-to-all-start
  315.8 2.9 fusion.108
  322.9 61.9 %all-to-all-done = bf16[1,256,8,768]{3,1,0,2:T(8,128)(2,1)S(1)} async-done(((bf16[1,256,8,768]{3,1,0,2:T(8,128)(2,1)}), bf16[1,256,8,768]{3,1,0,2:T(8,128)(2,1)S(1)}, u32[]{:S(2)}, u32[]{:S(2)}) %all-to-all-start) | async-done | bytes 3145760 | tf_op jit(solution)/shard_map/all_to_all | solution.py:180
  398.9 4.0 fusion.78
  402.9 3.7 copy.145
  406.6 4.4 all-to-all-start.1
  411.1 6.3 multiply_reduce_fusion
  418.3 2.6 multiply_convert_fusion
  426.7 5.0 multiply_bitcast_fusion
  447.6 6.9 fusion.75
  454.5 8.7 copy.162
  463.2 5.2 all-to-all-start.3
  470.5 8.1 fusion.91
  478.7 59.7 %all-to-all-done.3 = bf16[1,1024,2,768]{3,2,0,1:T(2,128)(2,1)} async-done(((bf16[1,1024,2,768]{3,2,0,1:T(2,128)(2,1)}), bf16[1,1024,2,768]{3,2,0,1:T(2,128)(2,1)}, u32[]{:S(2)}, u32[]{:S(2)}) %all-to-all-start.3) | async-done | bytes 3145760 | tf_op jit(solution)/shard_map/all_to_all | solution.py:240
  540.7 3.2 copy.164
  543.9 22.2 fusion.80
  566.2 44.0 %pad_maximum_fusion.1 = f32[8,1024,2048]{2,1,0:T(8,128)} fusion(f32[8,256,2048]{2,1,0:T(8,128)} %bitcast.187, f32[8,768,2048]{2,1,0:T(8,128)} %fusion.80), kind=kLoop, calls=%fused_computation.1 | loop fusion | flops 16777216 | bytes 134217728 | tf_op jit(solution)/shard_map/concatenate | solution.py:252
  611.3 23.0 convolution_add_fusion
  634.3 27.3 convert_reduce_fusion
  661.6 40.8 %fusion.121 = f32[8192,2048]{0,1:T(8,128)} fusion(bf16[256,8192]{1,0:T(8,128)(2,1)} %get-tuple-element.202, bf16[1,256,2048]{2,1,0:T(8,128)(2,1)S(1)} %copy-done.4, f32[2048]{0:T(1024)S(1)} %copy-done.50, f32[2048]{0:T(1024)S(1)} %copy-done.41, f32[256]{0:T(256)S(1)} %add_rsqrt_fusion, f32[256]{0:T(256)S(1)} %broadcast_multiply_fusion.5), kind=kOutput, calls=%fused_computation.178 | convolution fusion | flops 8593080320 | bytes 72370176 | tf_op jit(solution)/shard_map/dot_general | solution.py:29
  702.5 29.1 %fusion.89 = f32[8192,2048]{0,1:T(8,128)} fusion(bf16[1,256,2048]{2,1,0:T(8,128)(2,1)S(1)} %copy-done.15, f32[256,8192]{1,0:T(8,128)} %convolution_add_fusion), kind=kOutput, calls=%fused_computation.116 | convolution fusion | flops 8600420352 | bytes 76546048 | tf_op jit(solution)/shard_map/dot_general | solution.py:29
  731.5 91.1 %pad_maximum_fusion = f32[8192,4096]{0,1:T(8,128)} fusion(f32[8192,2048]{0,1:T(8,128)} %fusion.89, f32[8192,2048]{0,1:T(8,128)} %fusion.121), kind=kLoop, calls=%fused_computation | loop fusion | flops 33554432 | bytes 268435456 | tf_op jit(solution)/shard_map/concatenate | solution.py:208
  825.9 17.5 fusion.127
  843.4 13.8 fusion.61
  857.2 3.1 convert_reduce_fusion.3
  860.4 134.5 %reduce-scatter.3.cloned.1.call-done = f32[1024,2048]{1,0:T(8,128)} async-done(((f32[8192,2048]{1,0:T(8,128)}), f32[1024,2048]{1,0:T(8,128)}) %reduce-scatter.3.cloned.1.call-update) | async-done | bytes 8388624 | tf_op jit(solution)/shard_map/reduce_scatter | solution.py:251
  994.9 3.1 slice.138
  998.0 6.3 slice.137
  1004.3 735.3 %reduce-scatter.5.cloned.1.call-done = f32[1024,4096]{0,1:T(8,128)} async-done(((f32[8192,4096]{0,1:T(8,128)}), f32[1024,4096]{0,1:T(8,128)}) %reduce-scatter.5.cloned.1.call-update) | async-done | bytes 16777232 | tf_op jit(solution)/shard_map/reduce_scatter | solution.py:207
  1739.6 11.3 fusion.124
  1751.6 23.3 convolution_add_fusion.2
  1774.9 7.5 fusion.46
  1782.4 88.6 %all-reduce.5.cloned.1.call-done = (f32[2048]{0:T(1024)}, f32[2048]{0:T(1024)}, f32[2048]{0:T(1024)}, f32[2048]{0:T(1024)}, f32[6144]{0:T(1024)}, /*index=5*/f32[2048]{0:T(1024)}, f32[8192]{0:T(1024)}) async-done(((f32[2048]{0:T(1024)}, f32[2048]{0:T(1024)}, f32[2048]{0:T(1024)}, f32[2048]{0:T(1024)}, f32[6144]{0:T(1024)}, /*index=5*/f32[2048]{0:T(1024)}, f32[8192]{0:T(1024)}), (f32[2048]{0:T(1024)}, ...) | async-done | bytes 98320 | tf_op jit(solution)/shard_map/psum | solution.py:275
  1879.7 833.2 %all-reduce.7.cloned.1.call-done = (f32[768,2048]{1,0:T(8,128)}, f32[256,2048]{1,0:T(8,128)}, f32[1024,2048]{0,1:T(8,128)}, f32[1024,2048]{0,1:T(8,128)}) async-done(((f32[768,2048]{1,0:T(8,128)}, f32[256,2048]{1,0:T(8,128)}, f32[1024,2048]{0,1:T(8,128)}, f32[1024,2048]{0,1:T(8,128)}), (f32[768,2048]{1,0:T(8,128)}, f32[256,2048]{1,0:T(8,128)}, f32[1024,2048]{0,1:T(8,128)}, ...) | async-done | bytes 25165840 | tf_op jit(solution)/shard_map/psum | solution.py:261
  2712.9 9.1 copy.166
  2722.0 9.1 copy.167
  2731.7 6.4 copy.203
  (205 shorter events, 74.9 us)
Async XLA Ops:
  7.2 277.6 %all-gather.4.cloned.1.call-start = ((), (), s32[]{:S(2)}) async-start(), calls=%async_computation.6 | async-start | bytes 28311552 | tf_op jit(solution)/shard_map/all_gather | solution.py:173
  7.9 602.3 %all-gather.6.cloned.1.call-start = ((), (), s32[]{:S(2)}) async-start(), calls=%async_computation.7 | async-start | bytes 37748736 | tf_op jit(solution)/shard_map/all_gather | solution.py:197
  8.7 625.7 %all-gather.8.cloned.1.call-start = ((), (), s32[]{:S(2)}) async-start(), calls=%async_computation.8 | async-start | bytes 37748736 | tf_op jit(solution)/shard_map/all_gather | solution.py:198
  9.4 19.0 collective-permute-start
  28.4 79.1 %copy-start.9 = (bf16[256,2048]{1,0:T(8,128)(2,1)}, bf16[256,2048]{1,0:T(8,128)(2,1)S(1)}, u32[]{:S(2)}) copy-start(bf16[256,2048]{1,0:T(8,128)(2,1)S(1)} %collective-permute-done) | copy-start | bytes 3145732
  28.6 79.4 %copy-start.3 = (bf16[1,256,2048]{2,1,0:T(8,128)(2,1)S(1)}, bf16[1,256,2048]{2,1,0:T(8,128)(2,1)}, u32[]{:S(2)}) copy-start(bf16[1,256,2048]{2,1,0:T(8,128)(2,1)} %param.15) | copy-start | bytes 3145732
  28.6 75.6 %collective-permute-start.1 = (bf16[512,2048]{1,0:T(8,128)(2,1)S(1)}, bf16[512,2048]{1,0:T(8,128)(2,1)S(1)}, u32[]{:S(2)}, u32[]{:S(2)}) collective-permute-start(bf16[512,2048]{1,0:T(8,128)(2,1)S(1)} %pad_maximum_fusion.3), channel_id=1, source_target_pairs={{0,24},{4,28},{8,0},{12,4},{16,8},{20,12},{24,16},{28,20},{1,25},{... | collective-permute-start | bytes 6291464 | tf_op jit(solution)/shard_map/ppermute | solution.py:21
  107.5 159.9 %collective-permute-start.2 = (bf16[1024,2048]{1,0:T(8,128)(2,1)}, bf16[1024,2048]{1,0:T(8,128)(2,1)}, u32[]{:S(2)}, u32[]{:S(2)}) collective-permute-start(bf16[1024,2048]{1,0:T(8,128)(2,1)} %pad_maximum_fusion.2), channel_id=1, source_target_pairs={{0,16},{4,20},{8,24},{12,28},{16,0},{20,4},{24,8},{28,12},{1,17},{... | collective-permute-start | bytes 12582920 | tf_op jit(solution)/shard_map/ppermute | solution.py:21
  108.2 553.4 %copy-start.45 = (f32[256]{0:T(256)}, f32[256]{0:T(256)S(1)}, u32[]{:S(2)}) copy-start(f32[256]{0:T(256)S(1)} %broadcast_multiply_fusion.5) | copy-start | bytes 3076
  108.7 553.0 %copy-start.47 = (f32[256]{0:T(256)}, f32[256]{0:T(256)S(1)}, u32[]{:S(2)}) copy-start(f32[256]{0:T(256)S(1)} %add_rsqrt_fusion) | copy-start | bytes 3076
  110.2 160.6 %copy-start.8 = (bf16[256,2048]{1,0:T(8,128)(2,1)S(1)}, bf16[256,2048]{1,0:T(8,128)(2,1)}, u32[]{:S(2)}) copy-start(bf16[256,2048]{1,0:T(8,128)(2,1)} %param.23) | copy-start | bytes 3145732
  273.8 6.1 copy-start.40
  273.9 11.0 copy-start.43
  273.9 10.9 copy-start.49
  273.9 10.9 copy-start.53
  279.9 29.6 %all-to-all-start.2 = ((bf16[1,256,8,256]{1,3,0,2:T(8,128)(2,1)}), bf16[1,256,8,256]{1,3,0,2:T(8,128)(2,1)S(1)}, u32[]{:S(2)}, u32[]{:S(2)}) async-start(bf16[1,256,8,256]{1,3,0,2:T(8,128)(2,1)} %bitcast.23), calls=%async_computation.2 | async-start | bytes 2097152 | tf_op jit(solution)/shard_map/all_to_all | solution.py:222
  302.8 11.9 copy-start.39
  310.5 74.3 %all-to-all-start = ((bf16[1,256,8,768]{3,1,0,2:T(8,128)(2,1)}), bf16[1,256,8,768]{3,1,0,2:T(8,128)(2,1)S(1)}, u32[]{:S(2)}, u32[]{:S(2)}) async-start(bf16[1,256,8,768]{3,1,0,2:T(8,128)(2,1)} %copy.141), calls=%async_computation | async-start | bytes 6291456 | tf_op jit(solution)/shard_map/all_to_all | solution.py:180
  406.6 56.6 %all-to-all-start.1 = ((bf16[1,1024,2,256]{3,2,0,1:T(2,128)(2,1)}), bf16[1,1024,2,256]{3,2,0,1:T(2,128)(2,1)}, u32[]{:S(2)}, u32[]{:S(2)}) async-start(bf16[1,1024,2,256]{3,2,0,1:T(2,128)(2,1)} %copy.145), calls=%async_computation.1 | async-start | bytes 2097152 | tf_op jit(solution)/shard_map/all_to_all | solution.py:190
  411.0 6.3 slice-start
  411.0 7.0 slice-start.1
  411.1 7.2 copy-start.18
  418.3 4.6 copy-start.30
  418.3 4.6 copy-start.35
  426.7 9.9 copy-start.21
  439.6 5.4 copy-start.31
  441.0 5.7 copy-start.32
  441.0 6.6 copy-start.19
  463.2 7.3 copy-start.14
  463.2 75.2 %all-to-all-start.3 = ((bf16[1,1024,2,768]{3,2,0,1:T(2,128)(2,1)}), bf16[1,1024,2,768]{3,2,0,1:T(2,128)(2,1)}, u32[]{:S(2)}, u32[]{:S(2)}) async-start(bf16[1,1024,2,768]{3,2,0,1:T(2,128)(2,1)} %copy.162), calls=%async_computation.3 | async-start | bytes 6291456 | tf_op jit(solution)/shard_map/all_to_all | solution.py:240
  468.4 526.5 %reduce-scatter.3.cloned.1.call-start = ((), (), s32[]{:S(2)}) async-start(), calls=%async_computation.9 | async-start | bytes 75497472 | tf_op jit(solution)/shard_map/reduce_scatter | solution.py:251
  470.5 8.2 copy-start.26
  540.7 25.4 copy-start.1
  610.2 24.2 copy-start.15
  610.2 1129.4 %reduce-scatter.5.cloned.1.call-start = ((), (), s32[]{:S(2)}) async-start(), calls=%async_computation.10 | async-start | bytes 150994944 | tf_op jit(solution)/shard_map/reduce_scatter | solution.py:207
  822.7 1048.4 %all-reduce.5.cloned.1.call-start = ((), (), s32[]{:S(2)}) async-start(), calls=%async_computation.11 | async-start | bytes 196608 | tf_op jit(solution)/shard_map/psum | solution.py:275
  825.8 17.5 copy-start.5
  825.8 17.6 copy-start.11
  825.8 17.6 copy-start.42
  825.8 17.6 copy-start.44
  825.8 17.6 copy-start.46
  825.8 17.6 copy-start.48
  843.4 13.8 copy-start.16
  860.3 1852.5 %all-reduce.7.cloned.1.call-start = ((), (), s32[]{:S(2)}) async-start(), calls=%async_computation.12 | async-start | bytes 50331648 | tf_op jit(solution)/shard_map/psum | solution.py:261
  1751.6 23.3 copy-start.27
  1751.6 23.3 copy-start.55
  1873.1 858.0 %copy-start.51 = (f32[256]{0:T(256)}, f32[256]{0:T(256)S(1)}, u32[]{:S(2)}) copy-start(f32[256]{0:T(256)S(1)} %dynamic_slice.54) | copy-start | bytes 3076
  2731.7 6.4 copy-start.33
  (24 other events, 47.0 us)
Sparse Core Ops, SparseCore 0:
  9.9 241.9 all-gather.3
  253.8 161.5 all-gather.5
  417.3 160.7 all-gather.7
  610.3 384.5 reduce-scatter.2
  998.7 740.8 reduce-scatter.4
  1747.0 124.0 all-reduce.4
  1875.1 837.7 all-reduce.6
